TPU v7x, 32 devices: a whole 2x2x4 slice. The times are simulated.
32 devices in a mesh: section: 4 (over z), seq: 4 (over y, x), tp: 2 (over core).
Axes of the slice: x: 2, y: 2, z: 4, core: 2. Of those that a mesh axis runs over, the one named last changes fastest.
Arguments:
- queries: bfloat16 [4, 512, 8192], P('section', 'seq', 'tp'), may hold values from -64 to 64
- picture_key_matrix: bfloat16 [4, 32, 1024], P('section', ('seq', 'tp')), may hold values from -8 to 8
- picture_value_matrix: bfloat16 [4, 32, 1024], P('section', ('seq', 'tp')), may hold values from -6 to 6
- cotangent: bfloat16 [4, 512, 8192], P('section', 'seq', 'tp'), may hold values from -6 to 6
- pattern: int32 [4, 4, 4], P('section', 'seq'), may hold values from 0 to 1, as said below
- tile_owner: int32 [4, 4], P('section'), may hold values from 0 to 3, each once within a row
Outputs:
- attended: bfloat16 [4, 512, 8192], P('section', 'seq', 'tp')
- grad_queries: bfloat16 [4, 512, 8192], P('section', 'seq', 'tp')
- grad_keys: bfloat16 [4, 32, 1024], P('section', 'seq', 'tp')
- grad_values: bfloat16 [4, 32, 1024], P('section', 'seq', 'tp')
Inputs may be any that keep to these rules, and one draw needn't show every extreme that they name: `pattern`: every text block attends to at least one and at most four tiles. `tile_owner`: each slot's row is a permutation: every row block holds exactly one tile.
All inputs are finite; a program needn't handle non-finite values.
Results may differ from a plain program's by a relative error of at most 0.0092.
Values may be sent and summed in bfloat16 or wider, within the bound.
A program may use at most 64 MiB of HBM per device.

v0:
```python
import jax
import jax.numpy as jnp
from jax import lax
from jax.sharding import PartitionSpec as P

QUERY_HEADS = 64
KEY_VALUE_HEADS = 8
HEAD_SIZE = 128


def from_behind(block, axis, distance):
    devices = range(lax.axis_size(axis))
    route = [((i - distance) % len(devices), i) for i in devices]
    return lax.ppermute(block, axis, route)


def attend_group(query_group, key_group, value_group, cot_group, mask):
    scale = HEAD_SIZE ** (-0.5)
    scores = (
        jnp.einsum("thd,jd->htj", query_group, key_group, preferred_element_type=jnp.float32)
        * scale
    )
    scores = jnp.where(mask[None], scores, -jnp.inf)
    top = jnp.max(scores, axis=-1, keepdims=True)
    expo = jnp.exp(scores - top)
    probs = expo / jnp.sum(expo, axis=-1, keepdims=True)
    probs_low = probs.astype(jnp.bfloat16)
    out_low = jnp.einsum(
        "htj,jd->thd", probs_low, value_group, preferred_element_type=jnp.float32
    ).astype(jnp.bfloat16)
    delta = jnp.einsum("thd,thd->ht", cot_group, out_low, preferred_element_type=jnp.float32)
    dprobs = jnp.einsum("thd,jd->htj", cot_group, value_group, preferred_element_type=jnp.float32)
    ds_low = (probs * (dprobs - delta[:, :, None])).astype(jnp.bfloat16)
    grad_query = (
        jnp.einsum("htj,jd->thd", ds_low, key_group, preferred_element_type=jnp.float32) * scale
    ).astype(jnp.bfloat16)
    grad_key = (
        jnp.einsum("htj,thd->jd", ds_low, query_group, preferred_element_type=jnp.float32) * scale
    )
    grad_value = jnp.einsum("htj,thd->jd", probs_low, cot_group, preferred_element_type=jnp.float32)
    return (out_low, grad_query, grad_key, grad_value)


def run_heads(query_rows, cot_rows, key_table, value_table, mask):
    text_rows = query_rows.shape[0]
    head_group = QUERY_HEADS // KEY_VALUE_HEADS
    local_heads = key_table.shape[1] // HEAD_SIZE
    outs, grad_qs, grad_ks, grad_vs = ([], [], [], [])
    for key_value_head in range(local_heads):
        query_group = query_rows[
            :,
            key_value_head * head_group * HEAD_SIZE : (key_value_head + 1) * head_group * HEAD_SIZE,
        ].reshape(text_rows, head_group, HEAD_SIZE)
        cot_group = cot_rows[
            :,
            key_value_head * head_group * HEAD_SIZE : (key_value_head + 1) * head_group * HEAD_SIZE,
        ].reshape(text_rows, head_group, HEAD_SIZE)
        key_group = key_table[:, key_value_head * HEAD_SIZE : (key_value_head + 1) * HEAD_SIZE]
        value_group = value_table[:, key_value_head * HEAD_SIZE : (key_value_head + 1) * HEAD_SIZE]
        out_low, grad_query, grad_key, grad_value = attend_group(
            query_group, key_group, value_group, cot_group, mask
        )
        outs.append(out_low.reshape(text_rows, head_group * HEAD_SIZE))
        grad_qs.append(grad_query.reshape(text_rows, head_group * HEAD_SIZE))
        grad_ks.append(grad_key)
        grad_vs.append(grad_value)
    return (
        jnp.concatenate(outs, 1),
        jnp.concatenate(grad_qs, 1),
        jnp.concatenate(grad_ks, 1),
        jnp.concatenate(grad_vs, 1),
    )


def per_device(queries, picture_key_matrix, picture_value_matrix, cotangent, pattern, tile_owner):
    whole_keys, whole_values = (
        lax.all_gather(picture_key_matrix, ("seq", "tp"), axis=1, tiled=True),
        lax.all_gather(picture_value_matrix, ("seq", "tp"), axis=1, tiled=True),
    )
    col_width = picture_key_matrix.shape[2] // lax.axis_size("tp")
    col_start = lax.axis_index("tp") * col_width
    key_rows = lax.dynamic_slice_in_dim(whole_keys, col_start, col_width, 2)
    value_rows = lax.dynamic_slice_in_dim(whole_values, col_start, col_width, 2)
    upstream = from_behind(cotangent, "section", -1)
    tile_count = tile_owner.shape[1]
    hits = (tile_owner[0][:, None] == jnp.arange(tile_count, dtype=jnp.int32)[None, :]).astype(
        jnp.float32
    )
    block_hits = jnp.dot(pattern[0].astype(jnp.float32), hits) > 0.5
    text_rows = queries.shape[1]
    block_count = pattern.shape[1]
    tile_rows = key_rows.shape[1] // tile_count
    width = key_rows.shape[2]
    capacity = min(4 * block_count, tile_count)
    needed = jnp.max(block_hits.astype(jnp.int32), axis=0)
    order_key = (1 - needed) * tile_count + jnp.arange(tile_count, dtype=jnp.int32)
    selected_items = jnp.argsort(order_key)[:capacity]
    key_compact = (
        key_rows[0]
        .reshape(tile_count, tile_rows, width)[selected_items]
        .reshape(capacity * tile_rows, width)
    )
    value_compact = (
        value_rows[0]
        .reshape(tile_count, tile_rows, width)[selected_items]
        .reshape(capacity * tile_rows, width)
    )
    hits_compact = block_hits[:, selected_items]
    mask = jnp.broadcast_to(
        hits_compact[:, None, :, None], (block_count, text_rows // block_count, capacity, tile_rows)
    ).reshape(text_rows, capacity * tile_rows)
    attended, grad_queries, key_small, value_small = run_heads(
        queries[0], upstream[0], key_compact, value_compact, mask
    )
    empty = jnp.zeros((tile_count, tile_rows, width), jnp.float32)
    key_terms = (
        empty.at[selected_items]
        .set(key_small.reshape(capacity, tile_rows, width))
        .reshape(tile_count * tile_rows, width)
    )
    value_terms = (
        empty.at[selected_items]
        .set(value_small.reshape(capacity, tile_rows, width))
        .reshape(tile_count * tile_rows, width)
    )
    key_parts, value_parts = (
        lax.all_to_all(key_terms[None], "seq", split_axis=1, concat_axis=0, tiled=True),
        lax.all_to_all(value_terms[None], "seq", split_axis=1, concat_axis=0, tiled=True),
    )
    key_sums = jnp.sum(key_parts, axis=0, keepdims=True)
    value_sums = jnp.sum(value_parts, axis=0, keepdims=True)
    return (
        attended[None],
        grad_queries[None],
        key_sums.astype(jnp.bfloat16),
        value_sums.astype(jnp.bfloat16),
    )


def solution(mesh):
    in_specs = (
        P("section", "seq", "tp"),
        P("section", ("seq", "tp"), None),
        P("section", ("seq", "tp"), None),
        P("section", "seq", "tp"),
        P("section", "seq", None),
        P("section", None),
    )
    out_specs = (
        P("section", "seq", "tp"),
        P("section", "seq", "tp"),
        P("section", "seq", "tp"),
        P("section", "seq", "tp"),
    )
    return jax.shard_map(
        per_device, mesh=mesh, in_specs=in_specs, out_specs=out_specs, check_vma=False
    )
```

profile of v0, /device:TPU:0, one launch (start us, length us, event | category | flops | bytes accessed | tf_op | source)
XLA Modules:
  0.0 68.0 jit_solution(12976515537671493263)
XLA Ops:
  0.7 2.3 %copy.85 = bf16[1,128,4096]{1,2,0:T(8,128)(2,1)} copy(bf16[1,128,4096]{2,1,0:T(8,128)(2,1)} %param.9) | data formatting | bytes 2097152 | tf_op args[3]
  3.0 5.1 %collective-permute-start = (bf16[1,128,4096]{1,2,0:T(8,128)(2,1)}, bf16[1,128,4096]{1,2,0:T(8,128)(2,1)S(1)}, u32[]{:S(2)}, u32[]{:S(2)}) collective-permute-start(bf16[1,128,4096]{1,2,0:T(8,128)(2,1)} %copy.85), channel_id=1, source_target_pairs={{8,0},{16,8},{24,16},{0,24},{9,1},{17,9},{25,17},{1,25},{10,2},{18... | collective-permute-start | bytes 3145736 | tf_op jit(solution)/shard_map/ppermute | solution.py:14
  8.1 9.2 %all_gather.6 = bf16[1,32,1024]{2,0,1:T(2,128)(2,1)S(1)} all-gather(bf16[1,4,1024]{2,0,1:T(2,128)(2,1)S(1)} %copy.72), channel_id=1, replica_groups=mesh['section'=4,'seq'=4,'tp'=2] {'seq','tp'}, dimensions={1}, use_global_device_ids=true | all-gather | bytes 73728 | tf_op jit(solution)/shard_map/all_gather | solution.py:78
  17.3 9.2 %all_gather.7 = bf16[1,32,1024]{2,0,1:T(2,128)(2,1)S(1)} all-gather(bf16[1,4,1024]{2,0,1:T(2,128)(2,1)S(1)} %copy.74), channel_id=1, replica_groups=mesh['section'=4,'seq'=4,'tp'=2] {'seq','tp'}, dimensions={1}, use_global_device_ids=true | all-gather | bytes 73728 | tf_op jit(solution)/shard_map/all_gather | solution.py:77
  26.9 0.7 %sort.17 = (s32[4]{0:T(128)}, s32[4]{0:T(128)S(1)}) sort(s32[4]{0:T(128)S(1)} %get-tuple-element.24, s32[4]{0:T(128)S(1)} %iota.12), dimensions={0}, to_apply=%region_0.0 | sort | flops 8 | bytes 64 | tf_op jit(solution)/shard_map/jit(argsort)/sort | solution.py:97
  29.9 0.7 %fusion.62 = (f32[8,128]{1,0:T(8,128)S(1)}, f32[8,128,32]{1,2,0:T(8,128)}) fusion(f32[8,128,32]{1,2,0:T(8,128)S(1)} %fusion.31), kind=kOutput, calls=%fused_computation.117 | output fusion | flops 65567 | bytes 266240 | tf_op jit(solution)/shard_map/sub | solution.py:25
  31.4 0.7 %fusion.61 = (f32[8,128]{1,0:T(8,128)S(1)}, f32[8,128,32]{1,2,0:T(8,128)}) fusion(f32[8,128,32]{1,2,0:T(8,128)S(1)} %fusion.29), kind=kOutput, calls=%fused_computation.116 | output fusion | flops 65567 | bytes 266240 | tf_op jit(solution)/shard_map/sub | solution.py:25
  32.8 0.7 %fusion.60 = (f32[8,128]{1,0:T(8,128)S(1)}, f32[8,128,32]{1,2,0:T(8,128)}) fusion(f32[8,128,32]{1,2,0:T(8,128)S(1)} %fusion.27), kind=kOutput, calls=%fused_computation.115 | output fusion | flops 65567 | bytes 266240 | tf_op jit(solution)/shard_map/sub | solution.py:25
  34.1 0.8 %copy.82 = bf16[128,1024]{1,0:T(8,128)(2,1)} copy(bf16[128,1024]{0,1:T(8,128)(2,1)S(1)} %bitcast.239) | data formatting | bytes 524288 | tf_op jit(solution)/shard_map/reshape | solution.py:63
  34.9 0.8 %copy.83 = bf16[128,1024]{1,0:T(8,128)(2,1)} copy(bf16[128,1024]{0,1:T(8,128)(2,1)S(1)} %bitcast.240) | data formatting | bytes 524288 | tf_op jit(solution)/shard_map/reshape | solution.py:63
  36.4 0.9 %convolution_convert_fusion = bf16[128,8,128]{2,0,1:T(8,128)(2,1)S(1)} fusion(bf16[32,512]{1,0:T(8,128)(2,1)} %bitcast.267, f32[8,128]{1,0:T(8,128)S(1)} %get-tuple-element.26, f32[8,128,32]{1,2,0:T(8,128)S(1)} %fusion.25), kind=kOutput, calls=%fused_computation.13 | convolution fusion | flops 8619039 | bytes 536576 | tf_op jit(solution)/shard_map/htj,jd->thd/dot_general | solution.py:28
  37.4 0.8 %copy.84 = bf16[128,1024]{1,0:T(8,128)(2,1)} copy(bf16[128,1024]{0,1:T(8,128)(2,1)S(1)} %bitcast.241) | data formatting | bytes 524288 | tf_op jit(solution)/shard_map/reshape | solution.py:63
  38.2 2.2 %maximum_bitcast_fusion = bf16[1,128,4096]{2,1,0:T(8,128)(2,1)} fusion(bf16[128,1024]{1,0:T(8,128)(2,1)} %copy.84, bf16[128,1024]{1,0:T(8,128)(2,1)} %copy.83, bf16[128,1024]{1,0:T(8,128)(2,1)} %copy.82, bf16[128,1024]{1,0:T(8,128)(2,1)S(1)} %copy.81), kind=kLoop, calls=%fused_computation.71 | loop fusion | flops 4194304 | bytes 2097152 | tf_op jit(solution)/shard_map/broadcast_in_dim | solution.py:133
  40.4 1.8 %fusion.44 = (f32[8,128]{1,0:T(8,128)}, bf16[128,1024]{0,1:T(8,128)(2,1)}, f32[8,128]{1,0:T(8,128)}, bf16[128,1024]{0,1:T(8,128)(2,1)S(1)}, f32[8,128]{1,0:T(8,1...) fusion(bf16[128,8,128]{2,0,1:T(8,128)(2,1)S(1)} %convolution_convert_fusion.3, ...), kind=kLoop, calls=%fused_computation.80 | loop fusion | flops 2093056 | bytes 3162112 | tf_op jit(solution)/shard_map/thd,thd->ht/dot_general | solution.py:31
  42.2 1.3 %convolution_bitcast_fusion.7 = f32[32,128]{1,0:T(8,128)S(1)} fusion(bf16[128,8,128]{0,2,1:T(8,128)(2,1)} %bitcast.260, f32[8,128]{1,0:T(8,128)} %copy-done.15, f32[8,128,32]{1,2,0:T(8,128)} %copy-done.3), kind=kOutput, calls=%fused_computation.60 | convolution fusion | flops 8487967 | bytes 413696 | tf_op jit(solution)/shard_map/htj,thd->jd/dot_general | solution.py:40
  43.5 1.2 %fusion.35 = bf16[8,128,32]{1,2,0:T(8,128)(2,1)S(1)} fusion(bf16[128,8,128]{0,2,1:T(8,128)(2,1)} %bitcast.261, f32[8,128]{1,0:T(8,128)} %get-tuple-element.6, f32[8,128,32]{1,2,0:T(8,128)} %get-tuple-element.33, f32[8,128]{1,0:T(8,128)} %copy-done.15, bf16[32,512]{1,0:T(8,128)(2,1)} %bitcast.268), kind=kOutput, calls=%fused_computation.56 | convolution fusion | flops 8519680 | bytes 475136 | tf_op jit(solution)/shard_map/thd,jd->htj/dot_general | solution.py:32
  45.2 1.2 %convolution_bitcast_fusion.6 = f32[32,128]{1,0:T(8,128)S(1)} fusion(bf16[128,8,128]{0,2,1:T(8,128)(2,1)S(1)} %bitcast.258, f32[8,128]{1,0:T(8,128)S(1)} %get-tuple-element.30, f32[8,128,32]{1,2,0:T(8,128)} %copy-done.2), kind=kOutput, calls=%fused_computation.59 | convolution fusion | flops 8487967 | bytes 413696 | tf_op jit(solution)/shard_map/htj,thd->jd/dot_general | solution.py:40
  47.1 1.2 %convolution_bitcast_fusion.5 = f32[32,128]{1,0:T(8,128)S(1)} fusion(bf16[128,8,128]{0,2,1:T(8,128)(2,1)S(1)} %bitcast.256, f32[8,128]{1,0:T(8,128)S(1)} %get-tuple-element.28, f32[8,128,32]{1,2,0:T(8,128)} %copy-done.1), kind=kOutput, calls=%fused_computation.58 | convolution fusion | flops 8487967 | bytes 413696 | tf_op jit(solution)/shard_map/htj,thd->jd/dot_general | solution.py:40
  51.2 3.3 %all-to-all-start.1 = ((f32[1,32,512]{2,0,1:T(1,128)}), f32[1,32,512]{2,0,1:T(1,128)S(1)}, u32[]{:S(2)}, u32[]{:S(2)}) async-start(f32[1,32,512]{2,0,1:T(1,128)} %broadcast_in_dim_reshape.5), calls=%async_computation.1 | async-start | bytes 131072 | tf_op jit(solution)/shard_map/all_to_all | solution.py:128
  55.1 1.0 %maximum_bitcast_fusion.1 = bf16[1,128,4096]{2,1,0:T(8,128)(2,1)} fusion(bf16[128,1024]{1,0:T(8,128)(2,1)S(1)} %copy.93, bf16[128,1024]{1,0:T(8,128)(2,1)S(1)} %copy.92, bf16[128,1024]{1,0:T(8,128)(2,1)S(1)} %copy.91, bf16[128,1024]{1,0:T(8,128)(2,1)S(1)} %copy.90), kind=kLoop, calls=%fused_computation.72 | loop fusion | flops 4194304 | bytes 2097152 | tf_op jit(solution)/shard_map/broadcast_in_dim | solution.py:134
  56.8 0.7 %broadcast_in_dim_reshape.4 = f32[1,32,512]{2,0,1:T(1,128)} reshape(f32[4,8,512]{2,1,0:T(8,128)S(1)} %scatter_fusion) | data formatting | bytes 131072 | tf_op jit(solution)/shard_map/broadcast_in_dim;reshape | solution.py:127
  57.5 1.8 %all-to-all-done.1 = f32[1,32,512]{2,0,1:T(1,128)S(1)} async-done(((f32[1,32,512]{2,0,1:T(1,128)}), f32[1,32,512]{2,0,1:T(1,128)S(1)}, u32[]{:S(2)}, u32[]{:S(2)}) %all-to-all-start.1) | async-done | bytes 65568 | tf_op jit(solution)/shard_map/all_to_all | solution.py:128
  59.3 3.3 %all-to-all-start = ((f32[1,32,512]{2,0,1:T(1,128)}), f32[1,32,512]{2,0,1:T(1,128)S(1)}, u32[]{:S(2)}, u32[]{:S(2)}) async-start(f32[1,32,512]{2,0,1:T(1,128)} %broadcast_in_dim_reshape.4), calls=%async_computation | async-start | bytes 131072 | tf_op jit(solution)/shard_map/all_to_all | solution.py:127
  63.2 4.2 %all-to-all-done = f32[1,32,512]{2,0,1:T(1,128)S(1)} async-done(((f32[1,32,512]{2,0,1:T(1,128)}), f32[1,32,512]{2,0,1:T(1,128)S(1)}, u32[]{:S(2)}, u32[]{:S(2)}) %all-to-all-start) | async-done | bytes 65568 | tf_op jit(solution)/shard_map/all_to_all | solution.py:127
  (93 shorter events, 11.6 us)
Async XLA Ops:
  0.6 7.4 %copy-start.13 = (bf16[1,4,1024]{2,1,0:T(4,128)(2,1)S(1)}, bf16[1,4,1024]{2,1,0:T(4,128)(2,1)}, u32[]{:S(2)}) copy-start(bf16[1,4,1024]{2,1,0:T(4,128)(2,1)} %param.8) | copy-start | bytes 24580
  0.6 16.6 %copy-start.14 = (bf16[1,4,1024]{2,1,0:T(4,128)(2,1)S(1)}, bf16[1,4,1024]{2,1,0:T(4,128)(2,1)}, u32[]{:S(2)}) copy-start(bf16[1,4,1024]{2,1,0:T(4,128)(2,1)} %param.7) | copy-start | bytes 24580
  0.7 26.0 %copy-start.20 = (s32[1,4]{1,0:T(1,128)S(1)}, s32[1,4]{1,0:T(1,128)}, u32[]{:S(2)}) copy-start(s32[1,4]{1,0:T(1,128)} %param.11) | copy-start | bytes 52
  0.7 26.0 %copy-start.19 = (s32[1,1,4]{2,1,0:T(1,128)S(1)}, s32[1,1,4]{2,1,0:T(1,128)}, u32[]{:S(2)}) copy-start(s32[1,1,4]{2,1,0:T(1,128)} %param.10) | copy-start | bytes 52
  3.0 26.0 %copy-start = (bf16[1,128,4096]{2,1,0:T(8,128)(2,1)S(1)}, bf16[1,128,4096]{2,1,0:T(8,128)(2,1)}, u32[]{:S(2)}) copy-start(bf16[1,128,4096]{2,1,0:T(8,128)(2,1)} %param.6) | copy-start | bytes 3145732
  3.0 37.5 %collective-permute-start = (bf16[1,128,4096]{1,2,0:T(8,128)(2,1)}, bf16[1,128,4096]{1,2,0:T(8,128)(2,1)S(1)}, u32[]{:S(2)}, u32[]{:S(2)}) collective-permute-start(bf16[1,128,4096]{1,2,0:T(8,128)(2,1)} %copy.85), channel_id=1, source_target_pairs={{8,0},{16,8},{24,16},{0,24},{9,1},{17,9},{25,17},{1,25},{10,2},{18... | collective-permute-start | bytes 3145736 | tf_op jit(solution)/shard_map/ppermute | solution.py:14
  28.2 5.3 %copy-start.4 = (bf16[4,8,512]{2,1,0:T(8,128)(2,1)}, bf16[4,8,512]{2,1,0:T(8,128)(2,1)S(1)}, u32[]{:S(2)}) copy-start(bf16[4,8,512]{2,1,0:T(8,128)(2,1)S(1)} %gather_fusion.2) | copy-start | bytes 98308
  29.9 2.4 %copy-start.3 = (f32[8,128,32]{1,2,0:T(8,128)}, f32[8,128,32]{1,2,0:T(8,128)S(1)}, u32[]{:S(2)}) copy-start(f32[8,128,32]{1,2,0:T(8,128)S(1)} %fusion.31) | copy-start | bytes 393220
  30.6 2.1 %copy-start.15 = (f32[8,128]{1,0:T(8,128)}, f32[8,128]{1,0:T(8,128)S(1)}, u32[]{:S(2)}) copy-start(f32[8,128]{1,0:T(8,128)S(1)} %get-tuple-element.32) | copy-start | bytes 12292
  31.2 2.5 %copy-start.11 = (bf16[4,8,512]{2,1,0:T(8,128)(2,1)}, bf16[4,8,512]{2,1,0:T(8,128)(2,1)S(1)}, u32[]{:S(2)}) copy-start(bf16[4,8,512]{2,1,0:T(8,128)(2,1)S(1)} %gather_fusion) | copy-start | bytes 98308
  31.4 2.3 %copy-start.2 = (f32[8,128,32]{1,2,0:T(8,128)}, f32[8,128,32]{1,2,0:T(8,128)S(1)}, u32[]{:S(2)}) copy-start(f32[8,128,32]{1,2,0:T(8,128)S(1)} %fusion.29) | copy-start | bytes 393220
  32.8 1.2 %copy-start.1 = (f32[8,128,32]{1,2,0:T(8,128)}, f32[8,128,32]{1,2,0:T(8,128)S(1)}, u32[]{:S(2)}) copy-start(f32[8,128,32]{1,2,0:T(8,128)S(1)} %fusion.27) | copy-start | bytes 393220
  42.2 2.7 %copy-start.5 = (bf16[4,8,512]{2,1,0:T(8,128)(2,1)S(1)}, bf16[4,8,512]{2,1,0:T(8,128)(2,1)}, u32[]{:S(2)}) copy-start(bf16[4,8,512]{2,1,0:T(8,128)(2,1)} %copy-done.4) | copy-start | bytes 98308
  42.2 3.0 %copy-start.7 = (bf16[128,1024]{0,1:T(8,128)(2,1)S(1)}, bf16[128,1024]{0,1:T(8,128)(2,1)}, u32[]{:S(2)}) copy-start(bf16[128,1024]{0,1:T(8,128)(2,1)} %get-tuple-element.19) | copy-start | bytes 786436
  43.5 2.9 %copy-start.10 = (f32[8,128,32]{1,2,0:T(8,128)S(1)}, f32[8,128,32]{1,2,0:T(8,128)}, u32[]{:S(2)}) copy-start(f32[8,128,32]{1,2,0:T(8,128)} %get-tuple-element.31) | copy-start | bytes 393220
  43.5 2.9 %copy-start.12 = (bf16[4,8,512]{2,1,0:T(8,128)(2,1)S(1)}, bf16[4,8,512]{2,1,0:T(8,128)(2,1)}, u32[]{:S(2)}) copy-start(bf16[4,8,512]{2,1,0:T(8,128)(2,1)} %copy-done.11) | copy-start | bytes 98308
  43.5 2.9 %copy-start.18 = (f32[8,128]{1,0:T(8,128)S(1)}, f32[8,128]{1,0:T(8,128)}, u32[]{:S(2)}) copy-start(f32[8,128]{1,0:T(8,128)} %get-tuple-element.18) | copy-start | bytes 12292
  45.2 1.9 %copy-start.6 = (bf16[128,1024]{0,1:T(8,128)(2,1)S(1)}, bf16[128,1024]{0,1:T(8,128)(2,1)}, u32[]{:S(2)}) copy-start(bf16[128,1024]{0,1:T(8,128)(2,1)} %get-tuple-element.17) | copy-start | bytes 786436
  46.4 1.9 %copy-start.9 = (f32[8,128,32]{1,2,0:T(8,128)S(1)}, f32[8,128,32]{1,2,0:T(8,128)}, u32[]{:S(2)}) copy-start(f32[8,128,32]{1,2,0:T(8,128)} %get-tuple-element.29) | copy-start | bytes 393220
  46.4 1.9 %copy-start.17 = (f32[8,128]{1,0:T(8,128)S(1)}, f32[8,128]{1,0:T(8,128)}, u32[]{:S(2)}) copy-start(f32[8,128]{1,0:T(8,128)} %get-tuple-element.16) | copy-start | bytes 12292
  48.3 0.9 %copy-start.8 = (f32[8,128,32]{1,2,0:T(8,128)S(1)}, f32[8,128,32]{1,2,0:T(8,128)}, u32[]{:S(2)}) copy-start(f32[8,128,32]{1,2,0:T(8,128)} %get-tuple-element.27) | copy-start | bytes 393220
  48.3 0.9 %copy-start.16 = (f32[8,128]{1,0:T(8,128)S(1)}, f32[8,128]{1,0:T(8,128)}, u32[]{:S(2)}) copy-start(f32[8,128]{1,0:T(8,128)} %get-tuple-element.14) | copy-start | bytes 12292
  51.2 8.1 %all-to-all-start.1 = ((f32[1,32,512]{2,0,1:T(1,128)}), f32[1,32,512]{2,0,1:T(1,128)S(1)}, u32[]{:S(2)}, u32[]{:S(2)}) async-start(f32[1,32,512]{2,0,1:T(1,128)} %broadcast_in_dim_reshape.5), calls=%async_computation.1 | async-start | bytes 131072 | tf_op jit(solution)/shard_map/all_to_all | solution.py:128
  59.3 8.1 %all-to-all-start = ((f32[1,32,512]{2,0,1:T(1,128)}), f32[1,32,512]{2,0,1:T(1,128)S(1)}, u32[]{:S(2)}, u32[]{:S(2)}) async-start(f32[1,32,512]{2,0,1:T(1,128)} %broadcast_in_dim_reshape.4), calls=%async_computation | async-start | bytes 131072 | tf_op jit(solution)/shard_map/all_to_all | solution.py:127
where the time goes:
time: 68.5 us; the launch traced here: 68 us
  blocking collectives  18.4 us (27%)
  starting transfers between devices  11.6 us (17%)
  local copies, waits for them, and re-layouts  11.2 us (16%)
  matrix products  9.81 us (14%)
  other arithmetic  9.74 us (14%)
  waiting for transfers between devices  6.02 us (9%)
  between operations  1.2 us (2%)
    all_gather x1, blocking collectives, per_device(): lax.all_gather(picture_value_matrix, ('seq', 'tp'), axis=1, tiled=True)  9.22 us
    all_gather x1, blocking collectives, per_device(): lax.all_gather(picture_key_matrix, ('seq', 'tp'), axis=1, tiled=True)  9.19 us
    ppermute x1, starting transfers between devices, from_behind(): return lax.ppermute(block, axis, route)  5.08 us
    all_to_all x1, waiting for transfers between devices, per_device(): lax.all_to_all(key_terms[None], 'seq', split_axis=1, concat_axis=0, tiled...  4.21 us
    dot_general x4, matrix products, attend_group(): jnp.einsum('htj,thd->jd', probs_low, cot_group, preferred_element_type=jn...  3.85 us
    all_to_all x1, starting transfers between devices, per_device(): lax.all_to_all(key_terms[None], 'seq', split_axis=1, concat_axis=0, tiled...  3.28 us
    all_to_all x1, starting transfers between devices, per_device(): lax.all_to_all(value_terms[None], 'seq', split_axis=1, concat_axis=0, til...  3.28 us
    unnamed x48, local copies, waits for them, and re-layouts  3.13 us
  transfers between devices with their start and end apart: 3, of which 2 were waited for; matrix products, arithmetic and copies ran while one was open for 25% of the time, Pallas kernels for 0%

commit v1 on v0

v1 whole, which is shorter than its diff:
```python
import functools

import jax
import jax.numpy as jnp
from jax import lax
from jax.experimental import pallas as pl
from jax.experimental.pallas import tpu as pltpu
from jax.sharding import PartitionSpec as P

QUERY_HEADS = 64
KEY_VALUE_HEADS = 8
HEAD_SIZE = 128
FAN = QUERY_HEADS // KEY_VALUE_HEADS
PACK = 4
CUTS = 4
MESH = pl.DeviceIdType.MESH
F32 = jnp.float32
BF16 = jnp.bfloat16


def nt(a, b):
    return lax.dot_general(a, b, (((1,), (1,)), ((), ())), preferred_element_type=F32)


def nn(a, b):
    return lax.dot_general(a, b, (((1,), (0,)), ((), ())), preferred_element_type=F32)


def tn(a, b):
    return lax.dot_general(a, b, (((0,), (0,)), ((), ())), preferred_element_type=F32)


def kernel(
    nsec, nseq, ntp,
    q_hbm, k_hbm, v_hbm, c_hbm, pat, own,
    att_vm, gq_vm, gk_out, gv_out,
    q_vm, c_vm,
    kg, vg, ng, asm, k_bd, v_bd,
    p_f32, p_send, p_recv, dp_send, dp_recv,
    dk_t, dv_t, dk_r, dv_r,
    load_sem, own_sem,
    k_ss, k_rs, v_ss, v_rs, n_ss, n_rs,
    p_ss, p_rs, dp_ss, dp_rs,
    dk_ss, dk_rs, dv_ss, dv_rs,
):
    scale = HEAD_SIZE ** (-0.5)
    D = HEAD_SIZE
    n = nseq * ntp
    text, cols = q_vm.shape
    part = k_hbm.shape[1]
    width = k_hbm.shape[2] // ntp
    rows = part * n
    groups = width // D
    gcols = FAN * D
    share = rows // nseq
    sec, seq, tp = lax.axis_index("section"), lax.axis_index("seq"), lax.axis_index("tp")
    me = seq * ntp + tp
    up, down = lax.rem(sec + 1, nsec), lax.rem(sec + nsec - 1, nsec)

    def dev(s, i):
        return {"section": s, "seq": lax.div(i, ntp), "tp": lax.rem(i, ntp)}

    def half(i):
        return pl.ds(pl.multiple_of(lax.rem(i, ntp) * width, width), width)

    loads = [
        pltpu.make_async_copy(c_hbm.at[0], c_vm, load_sem.at[0]),
        pltpu.make_async_copy(q_hbm.at[0], q_vm, load_sem.at[1]),
    ]
    for c in loads:
        c.start()
    mine = [
        pltpu.make_async_copy(k_hbm.at[0, :, half(me)], kg.at[me], own_sem.at[0]),
        pltpu.make_async_copy(v_hbm.at[0, :, half(me)], vg.at[me], own_sem.at[1]),
    ]
    for c in mine:
        c.start()

    barrier = pltpu.get_barrier_semaphore()
    for d in range(n):
        peer = lax.rem(me + d, n)
        pl.semaphore_signal(barrier, inc=1, device_id=dev(up, peer), device_id_type=MESH)
        pl.semaphore_signal(barrier, inc=1, device_id=dev(down, peer), device_id_type=MESH)
        if d > 0:
            pl.semaphore_signal(barrier, inc=1, device_id=dev(sec, peer), device_id_type=MESH)

    row_tile = lax.broadcasted_iota(jnp.int32, (rows, text), 0) // (rows // own.shape[1])
    blocks = pat.shape[1]
    lane_block = lax.broadcasted_iota(jnp.int32, (rows, text), 1) // (text // blocks)
    allowed = jnp.zeros((rows, text), jnp.bool_)
    for b in range(blocks):
        for t in range(own.shape[1]):
            owner = jnp.where(pat[0, b, t] > 0, own[0, t], -1)
            hit = row_tile == owner
            if blocks > 1:
                hit = hit & (lane_block == b)
            allowed = allowed | hit
    k_bd[...] = jnp.zeros_like(k_bd)
    v_bd[...] = jnp.zeros_like(v_bd)

    pl.semaphore_wait(barrier, 3 * n - 1)

    def remote(src, dst, ss, rs, to):
        return pltpu.make_async_remote_copy(
            src_ref=src, dst_ref=dst, send_sem=ss, recv_sem=rs, device_id=to, device_id_type=MESH
        )

    n_copies, k_copies, v_copies = [], [], []
    for d in range(n):
        peer = lax.rem(me + d, n)
        c = remote(v_hbm.at[0, :, half(peer)], ng.at[me], n_ss.at[d], n_rs.at[d], dev(up, peer))
        c.start()
        n_copies.append(c)
    for d in range(1, n):
        peer = lax.rem(me + d, n)
        c = remote(k_hbm.at[0, :, half(peer)], kg.at[me], k_ss.at[d], k_rs.at[d], dev(sec, peer))
        c.start()
        k_copies.append(c)
    for d in range(1, n):
        peer = lax.rem(me + d, n)
        c = remote(v_hbm.at[0, :, half(peer)], vg.at[me], v_ss.at[d], v_rs.at[d], dev(sec, peer))
        c.start()
        v_copies.append(c)

    def assemble(which, src):
        for i in range(n):
            asm[which, part * i : part * (i + 1), :] = src[i].astype(F32)

    def head(ref, g, h):
        j = g * FAN + h
        return ref[:, j * D : (j + 1) * D]

    for c in mine + loads:
        c.wait()
    for c in k_copies:
        c.wait_recv()
    assemble(0, kg)
    keys = [asm[0, :, g * D : (g + 1) * D].astype(BF16) for g in range(groups)]
    p_copies, dp_copies = [], []

    def probs_of(g):
        for h in range(FAN):
            s = nt(keys[g], head(q_vm, g, h)) * scale
            s = jnp.where(allowed, s, -jnp.inf)
            e = jnp.exp(s - jnp.max(s, axis=0, keepdims=True))
            p = e * (1.0 / jnp.sum(e, axis=0, keepdims=True))
            p_f32[g, h * rows : (h + 1) * rows, :] = p
            p_send[g, h * rows : (h + 1) * rows, :] = p.astype(BF16)
        c = remote(
            p_send.at[g], p_recv.at[g], p_ss.at[g], p_rs.at[g], dev(up, me)
        )
        c.start()
        p_copies.append(c)

    def dprobs_of(g, values):
        for h in range(FAN):
            dp = nt(values, head(c_vm, g, h))
            dp = dp - jnp.sum(dp, axis=0, keepdims=True) * (1.0 / rows)
            dp_send[g, h * rows : (h + 1) * rows, :] = dp.astype(BF16)
        c = remote(
            dp_send.at[g], dp_recv.at[g], dp_ss.at[g], dp_rs.at[g], dev(down, me)
        )
        c.start()
        dp_copies.append(c)

    probs_of(0)
    for c in n_copies:
        c.wait_recv()
    assemble(1, ng)
    for g in range(groups):
        dprobs_of(g, asm[1, :, g * D : (g + 1) * D].astype(BF16))
        if g + 1 < groups:
            probs_of(g + 1)

    for c in v_copies:
        c.wait_recv()
    assemble(2, vg)
    for g in range(groups):
        values = asm[2, :, g * D : (g + 1) * D].astype(BF16)
        for a in range(PACK):
            k_bd[g, a * rows : (a + 1) * rows, a * D : (a + 1) * D] = keys[g]
            v_bd[g, a * rows : (a + 1) * rows, a * D : (a + 1) * D] = values

    lot = PACK * rows
    wide = PACK * D
    for g in range(groups):
        for a in range(FAN // PACK):
            at = g * gcols + a * wide
            o = tn(p_send[g, a * lot : (a + 1) * lot, :], v_bd[g])
            att_vm[0, :, at : at + wide] = o.astype(BF16)

    dk_copies, dv_copies = [], []
    for g in range(groups):
        dp_copies[g].wait_recv()
        dk = jnp.zeros((rows, D), F32)
        ds_list = []
        for h in range(FAN):
            at = slice(h * rows, (h + 1) * rows)
            p = p_f32[g, at, :]
            dp = dp_recv[g, at, :].astype(F32)
            delta = jnp.sum(p * dp, axis=0, keepdims=True)
            ds = (p * (dp - delta)).astype(BF16)
            ds_list.append(ds)
            dk = dk + nn(ds, head(q_vm, g, h))
        dk_t[g] = dk * scale
        for d in range(1, nseq):
            to = lax.rem(seq + d, nseq)
            c = remote(
                dk_t.at[g, pl.ds(pl.multiple_of(to * share, share), share), :],
                dk_r.at[d, g], dk_ss.at[g, d], dk_rs.at[g, d],
                {"section": sec, "seq": to, "tp": tp},
            )
            c.start()
            dk_copies.append(c)
        p_copies[g].wait_recv()
        dv = jnp.zeros((rows, D), F32)
        for h in range(FAN):
            dv = dv + nn(p_recv[g, h * rows : (h + 1) * rows, :], head(c_vm, g, h))
        dv_t[g] = dv
        for d in range(nseq):
            to = lax.rem(seq + d, nseq)
            c = remote(
                dv_t.at[g, pl.ds(pl.multiple_of(to * share, share), share), :],
                dv_r.at[d, g], dv_ss.at[g, d], dv_rs.at[g, d],
                {"section": down, "seq": to, "tp": tp},
            )
            c.start()
            dv_copies.append(c)
        for a in range(FAN // PACK):
            at = g * gcols + a * wide
            ds = jnp.concatenate(ds_list[a * PACK : (a + 1) * PACK], axis=0)
            gq_vm[0, :, at : at + wide] = (tn(ds, k_bd[g]) * scale).astype(BF16)

    for c in dk_copies + dv_copies:
        c.wait_recv()
    for g in range(groups):
        dk = dk_t[g, pl.ds(pl.multiple_of(seq * share, share), share), :]
        for d in range(1, nseq):
            dk = dk + dk_r[d, g]
        dv = dv_r[0, g]
        for d in range(1, nseq):
            dv = dv + dv_r[d, g]
        gk_out[0, :, g * D : (g + 1) * D] = dk.astype(BF16)
        gv_out[0, :, g * D : (g + 1) * D] = dv.astype(BF16)
    for c in n_copies + k_copies + v_copies + p_copies + dp_copies + dk_copies + dv_copies:
        c.wait_send()


def put_out(*refs):
    sems = refs[8]
    copies = []
    for i in range(4):
        step = refs[i].shape[1] // CUTS if i < 2 else refs[i].shape[1]
        for j in range(refs[i].shape[1] // step):
            at = slice(j * step, (j + 1) * step)
            copies.append(
                pltpu.make_async_copy(refs[i].at[:, at], refs[4 + i].at[:, at], sems.at[i, j])
            )
    for c in copies:
        c.start()
    for c in copies:
        c.wait()


def per_device(nsec, nseq, ntp, queries, keys, values, cotangent, pattern, tile_owner):
    n = nseq * ntp
    part = keys.shape[1]
    width = keys.shape[2] // ntp
    rows = part * n
    groups = width // HEAD_SIZE
    text, cols = queries.shape[1:]
    share = rows // nseq
    D = HEAD_SIZE
    dma = pltpu.SemaphoreType.DMA
    vm = pltpu.VMEM
    anyspace = pl.BlockSpec(memory_space=pl.ANY)
    smem = pl.BlockSpec(memory_space=pltpu.SMEM)
    vmem = pl.BlockSpec(memory_space=pltpu.VMEM)
    results = pl.pallas_call(
        functools.partial(kernel, nsec, nseq, ntp),
        out_shape=(
            vm((1, text, cols), BF16),
            vm((1, text, cols), BF16),
            vm((1, share, width), BF16),
            vm((1, share, width), BF16),
        ),
        in_specs=[anyspace] * 4 + [smem] * 2,
        out_specs=(vmem,) * 4,
        scratch_shapes=[
            vm((text, cols), BF16),
            vm((text, cols), BF16),
            vm((n, part, width), BF16),
            vm((n, part, width), BF16),
            vm((n, part, width), BF16),
            vm((3, rows, width), F32),
            vm((groups, PACK * rows, PACK * D), BF16),
            vm((groups, PACK * rows, PACK * D), BF16),
            vm((groups, FAN * rows, text), F32),
            vm((groups, FAN * rows, text), BF16),
            vm((groups, FAN * rows, text), BF16),
            vm((groups, FAN * rows, text), BF16),
            vm((groups, FAN * rows, text), BF16),
            vm((groups, rows, D), F32),
            vm((groups, rows, D), F32),
            vm((nseq, groups, share, D), F32),
            vm((nseq, groups, share, D), F32),
            dma((2,)),
            dma((2,)),
            dma((n,)), dma((n,)), dma((n,)), dma((n,)), dma((n,)), dma((n,)),
            dma((groups,)), dma((groups,)), dma((groups,)), dma((groups,)),
            dma((groups, nseq)), dma((groups, nseq)), dma((groups, nseq)), dma((groups, nseq)),
        ],
        compiler_params=pltpu.CompilerParams(collective_id=0, has_side_effects=True),
        name="cross",
    )(queries, keys, values, cotangent, pattern, tile_owner)
    return pl.pallas_call(
        put_out,
        out_shape=tuple(jax.ShapeDtypeStruct(r.shape, r.dtype) for r in results),
        in_specs=[vmem] * 4,
        out_specs=(anyspace,) * 4,
        scratch_shapes=[dma((4, CUTS))],
        name="put",
    )(*[pltpu.with_memory_space_constraint(r, pltpu.VMEM) for r in results])


def solution(mesh):
    nsec, nseq, ntp = (mesh.shape[a] for a in ("section", "seq", "tp"))
    in_specs = (
        P("section", "seq", "tp"),
        P("section", ("seq", "tp"), None),
        P("section", ("seq", "tp"), None),
        P("section", "seq", "tp"),
        P("section", "seq", None),
        P("section", None),
    )
    out_specs = (P("section", "seq", "tp"),) * 4
    return jax.shard_map(
        functools.partial(per_device, nsec, nseq, ntp),
        mesh=mesh, in_specs=in_specs, out_specs=out_specs, check_vma=False,
    )
```

time: 68.5 us -> 31.4 us (0.46)
  Pallas kernels: 0 us -> 30.6 us
  blocking collectives: 18.4 us -> 0 us
  starting transfers between devices: 11.6 us -> 0 us
  local copies, waits for them, and re-layouts: 11.2 us -> 0 us
  matrix products: 9.81 us -> 0 us
  other arithmetic: 9.74 us -> 0 us
  waiting for transfers between devices: 6.02 us -> 0 us
    pallas_call x0 -> x2, Pallas kernels: none -> 30.6 us  [the longest x1 29.1 us: per_device(): pl.pallas_call(functools.partial(kernel, nsec, nseq, ntp), out_shape=(vm(...]
    all_gather x2 -> x0, blocking collectives: 18.4 us -> none  [the longest x1 9.22 us: per_device(): lax.all_gather(picture_value_matrix, ('seq', 'tp'), axis=1, tiled=True)]
    dot_general x25 -> x0, matrix products: 9.81 us -> none  [the longest x4 3.85 us: attend_group(): jnp.einsum('htj,thd->jd', probs_low, cot_group, preferred_element_type=jn...]
    all_to_all x2 -> x0, starting transfers between devices: 6.56 us -> none  [the longest x1 3.28 us: per_device(): lax.all_to_all(key_terms[None], 'seq', split_axis=1, concat_axis=0, tiled...]
    all_to_all x2 -> x0, waiting for transfers between devices: 6.02 us -> none  [the longest x1 4.21 us: per_device(): lax.all_to_all(key_terms[None], 'seq', split_axis=1, concat_axis=0, tiled...]
    ppermute x1 -> x0, starting transfers between devices: 5.08 us -> none  [from_behind(): return lax.ppermute(block, axis, route)]
    reshape x8 -> x0, local copies, waits for them, and re-layouts: 3.26 us -> none  [the longest x4 2.68 us: run_heads(): outs.append(out_low.reshape(text_rows, head_group * HEAD_SIZE))]
    broadcast_in_dim x2 -> x0, other arithmetic: 3.2 us -> none  [the longest x1 2.16 us: per_device(): attended[None]]
  transfers between devices with their start and end apart: 3 -> 0, of which waited for: 2 -> 0; matrix products, arithmetic and copies ran while one was open for 25% -> 0% of each run, Pallas kernels for 0% -> 0%
where the time goes in v1:
time: 31.4 us; the launch traced here: 31.2 us
  Pallas kernels  30.6 us (97%)
  between operations  0.64 us (2%)
    pallas_call x1, Pallas kernels, per_device(): pl.pallas_call(functools.partial(kernel, nsec, nseq, ntp), out_shape=(vm(...  29.1 us
    pallas_call x1, Pallas kernels, per_device(): pl.pallas_call(put_out, out_shape=tuple((jax.ShapeDtypeStruct(r.shape, r....  1.45 us

profile of v1, /device:TPU:0, one launch (start us, length us, event | category | flops | bytes accessed | tf_op | source)
XLA Modules:
  0.0 31.2 jit_solution(17700583945524216638)
XLA Ops:
  0.6 29.1 %cross.1 = (bf16[1,128,4096]{2,1,0:T(8,128)(2,1)S(1)}, bf16[1,128,4096]{2,1,0:T(8,128)(2,1)S(1)}, bf16[1,8,512]{2,1,0:T(8,128)(2,1)S(1)}, bf16[1,8,512]{2,1,0:T(8,128)(2,1)S(1)}) custom-call(bf16[1,128,4096]{2,1,0:T(8,128)(2,1)} %q_hbm.1, bf16[1,4,1024]{2,1,0:T(4,128)(2,1)} %k_hbm.1, bf16[1,4,1024]{2,1,0:T(4,128)(2,1)} %v_hbm.1, ...), custom_call_target="tpu_custom_call" | custom-call | tf_op jit(solution)/shard_map/cross/pallas_call | solution.py:279
  29.7 1.5 %put.1 = (bf16[1,128,4096]{2,1,0:T(8,128)(2,1)}, bf16[1,128,4096]{2,1,0:T(8,128)(2,1)}, bf16[1,8,512]{2,1,0:T(8,128)(2,1)}, bf16[1,8,512]{2,1,0:T(8,128)(2,1)}) custom-call(bf16[1,128,4096]{2,1,0:T(8,128)(2,1)S(1)} %get-tuple-element.8.refs_0_, bf16[1,128,4096]{2,1,0:T(8,128)(2,1)S(1)} %get-tuple-element.9.refs_1_, ...), custom_call_target="tpu_custom_call" | custom-call | tf_op jit(solution)/shard_map/put/pallas_call | solution.py:316
